TPU v7x, 256 devices: a whole 4x4x8 slice. The times are simulated.
256 devices in a mesh: row: 8 (over y, x_lo), col: 32 (over x_hi, z, core).
Axes of the slice: x: 4 (x_hi: 2, x_lo: 2; x = x_hi * 2 + x_lo), y: 4, z: 8, core: 2. Of those that a mesh axis runs over, the one named last changes fastest.
Arguments:
- inv_sep: bfloat16 [24576, 24576], P('row', 'col'), may hold values from -6 to 6
- lower_one: bfloat16 [24576, 256], P('col', 'row'), may hold values from -0.0390625 to 0.0390625
- upper_one: bfloat16 [256, 24576], P('col', 'row'), may hold values from -0.0390625 to 0.0390625
- diag_inv_one: float32 [256, 256], replicated, may hold values from -6 to 6
- blocks_one: int32 [160], replicated, may hold values from 0 to 191, as said below
- lower_two: bfloat16 [24576, 256], P('col', 'row'), may hold values from -0.046875 to 0.046875
- upper_two: bfloat16 [256, 24576], P('col', 'row'), may hold values from -0.046875 to 0.046875
- corner_lower: bfloat16 [256, 256], replicated, may hold values from -0.375 to 0.375
- corner_upper: bfloat16 [256, 256], replicated, may hold values from -0.375 to 0.375
- diag_inv_two: float32 [256, 256], replicated, may hold values from -6 to 6
- blocks_two: int32 [128], replicated, may hold values from 0 to 191, as said below
Outputs:
- inv_lower_one: bfloat16 [20480, 256], P(('row', 'col'))
- inv_upper_one: bfloat16 [256, 20480], P('row', 'col')
- inv_diag_one: float32 [256, 256], replicated
- inv_lower_two: bfloat16 [16384, 256], P(('row', 'col'))
- inv_upper_two: bfloat16 [256, 16384], P('row', 'col')
- inv_diag_two: float32 [256, 256], replicated
Inputs may be any that keep to these rules, and one draw needn't show every extreme that they name: `blocks_one`: distinct block indices in increasing order; each aligned run of 6 blocks holds exactly 5 of them; the first and the last block of the separator are listed. `blocks_two`: distinct block indices in increasing order, each of them also in blocks_one; each aligned run of 6 blocks holds exactly 4 of them; the first and the last block of the separator are listed.
All inputs are finite; a program needn't handle non-finite values.
Results may differ from a plain program's by a relative error of at most 0.0039.
Values may be sent and summed in bfloat16 or wider, within the bound.
A program may use at most 64 MiB of HBM per device.

v0:
```python
import jax
import jax.numpy as jnp
from jax import lax
from jax.sharding import PartitionSpec as P

B = 128


def highest(first_mat, second_mat):
    return jnp.dot(
        first_mat.astype(jnp.float32),
        second_mat.astype(jnp.float32),
        precision=lax.Precision.HIGHEST,
    )


def take_rows(matrix, blocks):
    shaped = matrix.reshape(matrix.shape[0] // B, B, matrix.shape[1])
    return jnp.take(shaped, blocks, axis=0).reshape(blocks.shape[0] * B, matrix.shape[1])


def take_cols(matrix, blocks):
    shaped = matrix.reshape(matrix.shape[0], matrix.shape[1] // B, B)
    return jnp.take(shaped, blocks, axis=1).reshape(matrix.shape[0], blocks.shape[0] * B)


def block_rows(blocks):
    return (blocks[:, None] * B + jnp.arange(B, dtype=jnp.int32)[None, :]).reshape(-1)


def places(wanted, listed):
    return jnp.sum((listed[None, :] < wanted[:, None]).astype(jnp.int32), axis=1)


def on_device(
    inv_sep,
    lower_one,
    upper_one,
    diag_inv_one,
    blocks_one,
    lower_two,
    upper_two,
    corner_lower,
    corner_upper,
    diag_inv_two,
    blocks_two,
):
    row_index = lax.axis_index("row")
    col_index = lax.axis_index("col")
    row_count = lax.axis_size("row")
    col_count = lax.axis_size("col")
    rows_here, cols_here = inv_sep.shape
    panel_width = diag_inv_one.shape[0]
    run_blocks = cols_here // B
    pick_one = blocks_one.shape[0] // col_count
    pick_two = blocks_two.shape[0] // col_count
    runs_group = col_count // row_count
    group_one = pick_one * runs_group
    group_two = pick_two * runs_group
    share_one = pick_one * B // row_count
    share_two = pick_two * B // row_count
    upper_rows = panel_width // row_count
    row_one = lax.dynamic_slice_in_dim(blocks_one, row_index * group_one, group_one) - row_index * (
        rows_here // B
    )
    row_two = lax.dynamic_slice_in_dim(blocks_two, row_index * group_two, group_two) - row_index * (
        rows_here // B
    )
    col_one = (
        lax.dynamic_slice_in_dim(blocks_one, col_index * pick_one, pick_one)
        - col_index * run_blocks
    )
    col_two = (
        lax.dynamic_slice_in_dim(blocks_two, col_index * pick_two, pick_two)
        - col_index * run_blocks
    )
    sep_one = take_cols(take_rows(inv_sep, row_one), col_one)
    sep_two = take_cols(take_rows(inv_sep, row_two), col_two)
    lower_spots = block_rows(places(row_two, row_one))
    upper_spots = places(col_two, col_one)
    corner_mine = lax.dynamic_slice_in_dim(corner_upper, row_index * upper_rows, upper_rows, 1)
    lower_p = lax.all_gather(take_rows(lower_one, col_one), "row", axis=1, tiled=True)
    upper_p = lax.all_gather(take_cols(upper_one, row_one), "col", axis=0, tiled=True)
    inv_lower_one = lax.psum_scatter(
        -jnp.dot(sep_one, lower_p, preferred_element_type=jnp.float32),
        "col",
        scatter_dimension=0,
        tiled=True,
    ).astype(jnp.bfloat16)
    inv_upper_one = lax.psum_scatter(
        -jnp.dot(upper_p, sep_one, preferred_element_type=jnp.float32),
        "row",
        scatter_dimension=0,
        tiled=True,
    ).astype(jnp.bfloat16)
    lower_c = lax.all_gather(take_rows(lower_two, col_two), "row", axis=1, tiled=True)
    upper_c = lax.all_gather(take_cols(upper_two, row_two), "col", axis=0, tiled=True)
    own_rows = col_index * share_one + jnp.arange(share_one, dtype=jnp.int32)
    chooser = (lower_spots[:, None] == own_rows[None, :]).astype(jnp.float32)
    carried = jnp.dot(inv_lower_one, corner_lower, preferred_element_type=jnp.float32)
    direct = jnp.dot(sep_two, lower_c, preferred_element_type=jnp.float32)
    shifted_part = jnp.dot(chooser, carried, precision=lax.Precision.HIGHEST)
    inv_lower_two = lax.psum_scatter(
        -(direct + shifted_part), "col", scatter_dimension=0, tiled=True
    ).astype(jnp.bfloat16)
    ancestor_cols = take_cols(inv_upper_one, upper_spots)
    direct = jnp.dot(upper_c, sep_two, preferred_element_type=jnp.float32)
    shifted_part = jnp.dot(corner_mine, ancestor_cols, preferred_element_type=jnp.float32)
    inv_upper_two = lax.psum_scatter(
        -(direct + shifted_part), "row", scatter_dimension=0, tiled=True
    ).astype(jnp.bfloat16)
    upper_slab = lax.dynamic_slice_in_dim(upper_p, col_index * share_one, share_one, 1)
    second_slab = lax.dynamic_slice_in_dim(upper_c, col_index * share_two, share_two, 1)
    first_part = jnp.dot(upper_slab, inv_lower_one, preferred_element_type=jnp.float32)
    cross = jnp.dot(ancestor_cols, lower_c, preferred_element_type=jnp.float32)
    second_part = jnp.dot(second_slab, inv_lower_two, preferred_element_type=jnp.float32) - highest(
        corner_mine, cross
    )
    first_total = lax.psum(first_part, ("row", "col"))
    inv_diag_one = diag_inv_one - first_total
    second_total = lax.psum(second_part, ("row", "col"))
    tail_term = highest(corner_upper, highest(inv_diag_one, corner_lower))
    inv_diag_two = diag_inv_two - (second_total - tail_term)
    return (inv_lower_one, inv_upper_one, inv_diag_one, inv_lower_two, inv_upper_two, inv_diag_two)


def solution(mesh):
    return jax.shard_map(
        on_device,
        mesh=mesh,
        in_specs=(
            P("row", "col"),
            P("col", "row"),
            P("col", "row"),
            P(),
            P(),
            P("col", "row"),
            P("col", "row"),
            P(),
            P(),
            P(),
            P(),
        ),
        out_specs=(
            P(("row", "col"), None),
            P("row", "col"),
            P(),
            P(("row", "col"), None),
            P("row", "col"),
            P(),
        ),
        check_vma=False,
    )
```

profile of v0, /device:TPU:2, one launch (start us, length us, event | category | flops | bytes accessed | tf_op | source)
XLA Modules:
  0.0 767.2 jit_solution(17721407719966944696)
XLA Ops:
  7.2 0.8 compare_and_fusion.3
  8.1 1.4 gather_fusion.3
  9.5 0.6 bitcast_select_fusion.3
  10.2 5.3 gather_fusion
  15.5 9.2 %reshape.206 = bf16[2560,6,128]{2,1,0:T(8,128)(2,1)} reshape(bf16[20,128,768]{2,1,0:T(8,128)(2,1)} %gather_fusion) | data formatting | bytes 7864320 | tf_op jit(solution)/shard_map/jit(_take)/gather | solution.py:19
  24.7 5.2 copy_select_fusion
  30.0 3.3 gather_fusion.1
  33.3 3.4 copy.41
  36.8 0.6 gather_fusion.2
  37.4 29.7 %all_gather.12 = bf16[640,256]{0,1:T(8,128)(2,1)S(1)} all-gather(bf16[640,32]{0,1:T(8,128)(2,1)S(1)} %bitcast_select_fusion.2), channel_id=1, replica_groups=mesh['row'=8,'col'=32] {'row'}, dimensions={1}, use_global_device_ids=true | all-gather | bytes 368640 | tf_op jit(solution)/shard_map/all_gather | solution.py:82
  67.2 2.3 bitcast_select_fusion
  69.5 2.8 convolution_negate_fusion
  72.3 19.8 %all-gather.3.cloned.1.call-done = bf16[256,2560]{1,0:T(8,128)(2,1)} async-done(((bf16[8,2560]{1,0:T(8,128)(2,1)}), bf16[256,2560]{1,0:T(8,128)(2,1)}) %all-gather.3.cloned.1.call-update) | async-done | bytes 1310736 | tf_op jit(solution)/shard_map/all_gather | solution.py:83
  92.1 3.4 convolution_negate_fusion.1
  95.8 0.6 gather_fusion.7
  96.4 0.6 bitcast_select_fusion.6
  97.1 3.1 gather_fusion.4
  100.2 0.2 convert_reduce_fusion
  100.4 4.6 reshape.207
  105.0 2.8 copy_select_fusion.1
  108.1 0.6 gather_fusion.6
  108.6 2.2 gather_fusion.5
  110.8 4.0 copy.46
  114.8 28.8 %all_gather.14 = bf16[512,256]{0,1:T(8,128)(2,1)S(1)} all-gather(bf16[512,32]{0,1:T(8,128)(2,1)S(1)} %bitcast_select_fusion.5), channel_id=1, replica_groups=mesh['row'=8,'col'=32] {'row'}, dimensions={1}, use_global_device_ids=true | all-gather | bytes 294912 | tf_op jit(solution)/shard_map/all_gather | solution.py:96
  143.7 2.1 bitcast_select_fusion.1
  145.8 2.1 fusion.24
  147.9 66.1 %reduce-scatter.5.cloned.1.call-done = f32[80,256]{1,0:T(8,128)} async-done(((f32[2560,256]{1,0:T(8,128)}), f32[80,256]{1,0:T(8,128)}) %reduce-scatter.5.cloned.1.call-update) | async-done | bytes 81936 | tf_op jit(solution)/shard_map/reduce_scatter | solution.py:84
  213.9 0.9 convert_element_type.22
  215.0 3.5 fusion
  218.6 0.2 convert_reduce_fusion.1
  218.9 35.1 %reduce-scatter.7.cloned.1.call-done = f32[32,640]{1,0:T(8,128)} async-done(((f32[256,640]{1,0:T(8,128)}), f32[32,640]{1,0:T(8,128)}) %reduce-scatter.7.cloned.1.call-update) | async-done | bytes 81936 | tf_op jit(solution)/shard_map/reduce_scatter | solution.py:90
  253.9 0.9 copy_bitcast_fusion.2
  254.8 0.6 gather_fusion.8
  255.4 0.3 fusion.12
  255.7 80.1 %all-gather.5.cloned.1.call-done = bf16[256,2048]{1,0:T(8,128)(2,1)} async-done(((bf16[8,2048]{1,0:T(8,128)(2,1)}), bf16[256,2048]{1,0:T(8,128)(2,1)}) %all-gather.5.cloned.1.call-update) | async-done | bytes 1048592 | tf_op jit(solution)/shard_map/all_gather | solution.py:97
  335.8 2.8 fusion.1
  338.9 1.9 fusion.9
  340.7 115.8 %reduce-scatter.9.cloned.1.call-done = f32[64,256]{1,0:T(8,128)} async-done(((f32[2048,256]{1,0:T(8,128)}), f32[64,256]{1,0:T(8,128)}) %reduce-scatter.9.cloned.1.call-update) | async-done | bytes 65552 | tf_op jit(solution)/shard_map/reduce_scatter | solution.py:103
  456.5 0.8 convert_element_type.25
  457.4 1.1 fusion.7
  458.5 1.0 convolution_subtract_fusion
  459.5 0.6 convert_element_type.23
  460.2 35.7 %reduce-scatter.11.cloned.1.call-done = f32[32,512]{1,0:T(8,128)} async-done(((f32[256,512]{1,0:T(8,128)}), f32[32,512]{1,0:T(8,128)}) %reduce-scatter.11.cloned.1.call-update) | async-done | bytes 65552 | tf_op jit(solution)/shard_map/reduce_scatter | solution.py:109
  495.8 1.5 convert_element_type.27
  497.3 259.8 %all-reduce.3.cloned.1.call-done = (f32[256,256]{1,0:T(8,128)}, f32[256,256]{1,0:T(8,128)}) async-done(((f32[256,256]{1,0:T(8,128)}, f32[256,256]{1,0:T(8,128)}), (f32[256,256]{1,0:T(8,128)}, f32[256,256]{1,0:T(8,128)})) %all-reduce.3.cloned.1.call-update) | async-done | bytes 524304 | tf_op jit(solution)/shard_map/psum | solution.py:119
  757.1 1.0 sub.40
  758.1 0.3 fusion.26
  758.4 2.0 fusion.3
  (68 shorter events, 1.6 us)
Async XLA Ops:
  7.2 248.2 %copy-start = (bf16[256,256]{1,0:T(8,128)(2,1)S(1)}, bf16[256,256]{1,0:T(8,128)(2,1)}, u32[]{:S(2)}) copy-start(bf16[256,256]{1,0:T(8,128)(2,1)} %param.19) | copy-start | bytes 393220
  7.2 85.0 %all-gather.3.cloned.1.call-start = ((), (), s32[]{:S(2)}) async-start(), calls=%async_computation.5 | async-start | bytes 1351680 | tf_op jit(solution)/shard_map/all_gather | solution.py:83
  10.1 203.8 %reduce-scatter.5.cloned.1.call-start = ((), (), s32[]{:S(2)}) async-start(), calls=%async_computation.4 | async-start | bytes 2703360 | tf_op jit(solution)/shard_map/reduce_scatter | solution.py:84
  24.7 5.2 copy-start.12
  33.3 3.4 copy-start.8
  72.3 23.4 %copy-start.11 = (s32[128]{0:T(128)S(1)}, s32[128]{0:T(128)}, u32[]{:S(2)}) copy-start(s32[128]{0:T(128)} %param.21) | copy-start | bytes 1540
  72.3 23.5 %copy-start.10 = (bf16[8,3072]{1,0:T(8,128)(2,1)S(1)}, bf16[8,3072]{1,0:T(8,128)(2,1)}, u32[]{:S(2)}) copy-start(bf16[8,3072]{1,0:T(8,128)(2,1)} %param.17) | copy-start | bytes 147460
  72.3 181.6 %reduce-scatter.7.cloned.1.call-start = ((), (), s32[]{:S(2)}) async-start(), calls=%async_computation.6 | async-start | bytes 737280 | tf_op jit(solution)/shard_map/reduce_scatter | solution.py:90
  95.6 240.2 %all-gather.5.cloned.1.call-start = ((), (), s32[]{:S(2)}) async-start(), calls=%async_computation.8 | async-start | bytes 1081344 | tf_op jit(solution)/shard_map/all_gather | solution.py:97
  97.1 359.5 %reduce-scatter.9.cloned.1.call-start = ((), (), s32[]{:S(2)}) async-start(), calls=%async_computation.7 | async-start | bytes 2162688 | tf_op jit(solution)/shard_map/reduce_scatter | solution.py:103
  105.0 3.0 copy-start.9
  145.8 69.1 %copy-start.2 = (bf16[256,256]{1,0:T(8,128)(2,1)S(1)}, bf16[256,256]{1,0:T(8,128)(2,1)}, u32[]{:S(2)}) copy-start(bf16[256,256]{1,0:T(8,128)(2,1)} %param.18) | copy-start | bytes 393220
  214.8 124.0 %copy-start.3 = (bf16[80,256]{1,0:T(8,128)(2,1)}, bf16[80,256]{1,0:T(8,128)(2,1)S(1)}, u32[]{:S(2)}) copy-start(bf16[80,256]{1,0:T(8,128)(2,1)S(1)} %convert_element_type.22) | copy-start | bytes 122884
  218.5 277.3 %reduce-scatter.11.cloned.1.call-start = ((), (), s32[]{:S(2)}) async-start(), calls=%async_computation.9 | async-start | bytes 589824 | tf_op jit(solution)/shard_map/reduce_scatter | solution.py:109
  255.7 203.9 %copy-start.4 = (f32[32,640]{1,0:T(8,128)S(1)}, f32[32,640]{1,0:T(8,128)}, u32[]{:S(2)}) copy-start(f32[32,640]{1,0:T(8,128)} %reduce-scatter.7.cloned.1.call-done) | copy-start | bytes 245764
  338.6 418.5 %copy-start.5 = (f32[256,256]{1,0:T(8,128)S(1)}, f32[256,256]{1,0:T(8,128)}, u32[]{:S(2)}) copy-start(f32[256,256]{1,0:T(8,128)} %param.14) | copy-start | bytes 786436
  338.6 419.8 %copy-start.6 = (f32[256,256]{1,0:T(8,128)S(1)}, f32[256,256]{1,0:T(8,128)}, u32[]{:S(2)}) copy-start(f32[256,256]{1,0:T(8,128)} %param.20) | copy-start | bytes 786436
  338.6 418.5 %all-reduce.3.cloned.1.call-start = ((), (), s32[]{:S(2)}) async-start(), calls=%async_computation.10 | async-start | bytes 1048576 | tf_op jit(solution)/shard_map/psum | solution.py:119
  457.4 303.0 %copy-start.7 = (bf16[64,256]{1,0:T(8,128)(2,1)}, bf16[64,256]{1,0:T(8,128)(2,1)S(1)}, u32[]{:S(2)}) copy-start(bf16[64,256]{1,0:T(8,128)(2,1)S(1)} %convert_element_type.25) | copy-start | bytes 98308
  758.1 2.3 copy-start.1
Sparse Core Ops, SparseCore 0:
  11.4 80.7 all-gather.2
  96.3 117.6 reduce-scatter.4
  216.6 37.2 reduce-scatter.6
  257.5 78.2 all-gather.4
  340.3 116.1 reduce-scatter.8
  458.9 36.8 reduce-scatter.10
  502.9 254.1 all-reduce.2
where the time goes:
time: 768 us; the launch traced here: 767 us
  waiting for transfers between devices  612 us (80%)
  blocking collectives  58.5 us (8%)
  local copies, waits for them, and re-layouts  39.2 us (5%)
  matrix products  21.4 us (3%)
  other arithmetic  20.9 us (3%)
  between operations  14.4 us (2%)
    psum x1, waiting for transfers between devices, on_device(): first_total = lax.psum(first_part, ('row', 'col'))  260 us
    reduce_scatter x1, waiting for transfers between devices, on_device(): lax.psum_scatter(-(direct + shifted_part), 'col', scatter_dimension=0, ti...  116 us
    all_gather x1, waiting for transfers between devices, on_device(): lax.all_gather(take_cols(upper_two, row_two), 'col', axis=0, tiled=True)  80.1 us
    reduce_scatter x1, waiting for transfers between devices, on_device(): lax.psum_scatter(-jnp.dot(sep_one, lower_p, preferred_element_type=jnp.fl...  66.1 us
    reduce_scatter x1, waiting for transfers between devices, on_device(): lax.psum_scatter(-(direct + shifted_part), 'row', scatter_dimension=0, ti...  35.7 us
    reduce_scatter x1, waiting for transfers between devices, on_device(): lax.psum_scatter(-jnp.dot(upper_p, sep_one, preferred_element_type=jnp.fl...  35.1 us
    all_gather x1, blocking collectives, on_device(): lax.all_gather(take_rows(lower_one, col_one), 'row', axis=1, tiled=True)  29.7 us
    all_gather x1, blocking collectives, on_device(): lax.all_gather(take_rows(lower_two, col_two), 'row', axis=1, tiled=True)  28.8 us
  transfers between devices with their start and end apart: 7, of which 7 were waited for; matrix products, arithmetic and copies ran while one was open for 10% of the time, Pallas kernels for 0%

commit v1 on v0

--- a/solution.py
+++ b/solution.py
@@ -116,7 +116,9 @@
     second_part = jnp.dot(second_slab, inv_lower_two, preferred_element_type=jnp.float32) - highest(
         corner_mine, cross
     )
-    first_total = lax.psum(first_part, ("row", "col"))
+    first_total = first_part
+    for kk in ("row", "col"):
+        first_total = lax.psum(first_total, kk)
     inv_diag_one = diag_inv_one - first_total
     second_total = lax.psum(second_part, ("row", "col"))
     tail_term = highest(corner_upper, highest(inv_diag_one, corner_lower))

time: 768 us -> 1170 us (1.52)
  waiting for transfers between devices: 612 us -> 1010 us
    psum x1 -> x3, waiting for transfers between devices: 260 us -> 537 us  [the longest x2 280 us: on_device(): first_total = lax.psum(first_total, kk)]
    all_gather x1, waiting for transfers between devices: 19.8 us -> 79.1 us  [on_device(): lax.all_gather(take_cols(upper_one, row_one), 'col', axis=0, tiled=True)]
    reduce_scatter x1, waiting for transfers between devices: 66.1 us -> 121 us  [on_device(): lax.psum_scatter(-jnp.dot(sep_one, lower_p, preferred_element_type=jnp.fl...]
  transfers between devices with their start and end apart: 7 -> 9, of which waited for: 7 -> 9; matrix products, arithmetic and copies ran while one was open for 10% -> 4% of each run, Pallas kernels for 0% -> 0%
where the time goes in v1:
time: 1170 us
  waiting for transfers between devices  1010 us (86%)
  blocking collectives  58.3 us (5%)
  local copies, waits for them, and re-layouts  38.4 us (3%)
  matrix products  21.3 us (2%)
  other arithmetic  20.7 us (2%)
  between operations  14.1 us (1%)
    psum x2, waiting for transfers between devices, on_device(): first_total = lax.psum(first_total, kk)  280 us
    psum x1, waiting for transfers between devices, on_device(): second_total = lax.psum(second_part, ('row', 'col'))  257 us
    reduce_scatter x1, waiting for transfers between devices, on_device(): lax.psum_scatter(-jnp.dot(sep_one, lower_p, preferred_element_type=jnp.fl...  121 us
    reduce_scatter x1, waiting for transfers between devices, on_device(): lax.psum_scatter(-(direct + shifted_part), 'col', scatter_dimension=0, ti...  121 us
    all_gather x1, waiting for transfers between devices, on_device(): lax.all_gather(take_cols(upper_two, row_two), 'col', axis=0, tiled=True)  79.7 us
    all_gather x1, waiting for transfers between devices, on_device(): lax.all_gather(take_cols(upper_one, row_one), 'col', axis=0, tiled=True)  79.1 us
    reduce_scatter x1, waiting for transfers between devices, on_device(): lax.psum_scatter(-jnp.dot(upper_p, sep_one, preferred_element_type=jnp.fl...  38.4 us
    reduce_scatter x1, waiting for transfers between devices, on_device(): lax.psum_scatter(-(direct + shifted_part), 'row', scatter_dimension=0, ti...  36 us
  transfers between devices with their start and end apart: 9, of which 9 were waited for; matrix products, arithmetic and copies ran while one was open for 4% of the time, Pallas kernels for 0%

profile of v1, /device:TPU:2, one launch (start us, length us, event | category | flops | bytes accessed | tf_op | source)
XLA Modules:
  0.0 1166.6 jit_solution(13566333004282500684)
XLA Ops:
  7.2 0.8 compare_and_fusion.3
  8.0 5.3 gather_fusion
  13.3 9.2 reshape.206
  22.7 5.3 copy_select_fusion
  28.0 3.3 gather_fusion.1
  31.3 3.4 copy.41
  34.8 0.6 gather_fusion.2
  35.4 2.3 bitcast_select_fusion
  37.7 29.5 %all_gather.12 = bf16[640,256]{0,1:T(8,128)(2,1)S(1)} all-gather(bf16[640,32]{0,1:T(8,128)(2,1)S(1)} %bitcast_select_fusion.2), channel_id=1, replica_groups=mesh['row'=8,'col'=32] {'row'}, dimensions={1}, use_global_device_ids=true | all-gather | bytes 368640 | tf_op jit(solution)/shard_map/all_gather | solution.py:82
  67.2 2.7 convolution_negate_fusion
  70.0 0.6 gather_fusion.3
  70.6 0.6 bitcast_select_fusion.3
  71.3 121.5 %reduce-scatter.5.cloned.1.call-done = f32[80,256]{1,0:T(8,128)} async-done(((f32[2560,256]{1,0:T(8,128)}), f32[80,256]{1,0:T(8,128)}) %reduce-scatter.5.cloned.1.call-update) | async-done | bytes 81936 | tf_op jit(solution)/shard_map/reduce_scatter | solution.py:84
  192.7 0.9 convert_element_type.22
  193.6 79.1 %all-gather.3.cloned.1.call-done = bf16[256,2560]{1,0:T(8,128)(2,1)} async-done(((bf16[8,2560]{1,0:T(8,128)(2,1)}), bf16[256,2560]{1,0:T(8,128)(2,1)}) %all-gather.3.cloned.1.call-update) | async-done | bytes 1310736 | tf_op jit(solution)/shard_map/all_gather | solution.py:83
  272.7 1.8 fusion.9
  274.6 3.4 convolution_negate_fusion.1
  278.2 0.6 gather_fusion.7
  278.9 0.6 bitcast_select_fusion.6
  279.6 3.1 gather_fusion.4
  282.7 4.7 reshape.207
  287.4 2.8 copy_select_fusion.1
  290.3 2.2 gather_fusion.5
  292.5 4.0 copy.46
  296.5 0.6 gather_fusion.6
  297.2 28.8 %all_gather.14 = bf16[512,256]{0,1:T(8,128)(2,1)S(1)} all-gather(bf16[512,32]{0,1:T(8,128)(2,1)S(1)} %bitcast_select_fusion.5), channel_id=1, replica_groups=mesh['row'=8,'col'=32] {'row'}, dimensions={1}, use_global_device_ids=true | all-gather | bytes 294912 | tf_op jit(solution)/shard_map/all_gather | solution.py:96
  326.1 1.8 bitcast_select_fusion.1
  328.0 2.1 fusion.24
  330.2 20.3 %all-reduce.4.cloned.1.call-done = f32[256,256]{1,0:T(8,128)} async-done(((f32[256,256]{1,0:T(8,128)}), f32[256,256]{1,0:T(8,128)}) %all-reduce.4.cloned.1.call-update) | async-done | bytes 262160 | tf_op jit(solution)/shard_map/psum | solution.py:121
  350.6 3.5 fusion
  354.5 38.4 %reduce-scatter.7.cloned.1.call-done = f32[32,640]{1,0:T(8,128)} async-done(((f32[256,640]{1,0:T(8,128)}), f32[32,640]{1,0:T(8,128)}) %reduce-scatter.7.cloned.1.call-update) | async-done | bytes 81936 | tf_op jit(solution)/shard_map/reduce_scatter | solution.py:90
  392.9 1.0 copy_bitcast_fusion.2
  393.9 0.6 gather_fusion.8
  394.4 0.3 fusion.12
  394.7 79.7 %all-gather.5.cloned.1.call-done = bf16[256,2048]{1,0:T(8,128)(2,1)} async-done(((bf16[8,2048]{1,0:T(8,128)(2,1)}), bf16[256,2048]{1,0:T(8,128)(2,1)}) %all-gather.5.cloned.1.call-update) | async-done | bytes 1048592 | tf_op jit(solution)/shard_map/all_gather | solution.py:97
  474.4 2.8 fusion.1
  477.3 0.6 convert_element_type.23
  478.1 259.5 %all-reduce.6.cloned.1.call-done = f32[256,256]{1,0:T(8,128)} async-done(((f32[256,256]{1,0:T(8,128)}), f32[256,256]{1,0:T(8,128)}) %all-reduce.6.cloned.1.call-update) | async-done | bytes 262160 | tf_op jit(solution)/shard_map/psum | solution.py:121
  737.6 1.0 sub.40
  738.6 121.4 %reduce-scatter.9.cloned.1.call-done = f32[64,256]{1,0:T(8,128)} async-done(((f32[2048,256]{1,0:T(8,128)}), f32[64,256]{1,0:T(8,128)}) %reduce-scatter.9.cloned.1.call-update) | async-done | bytes 65552 | tf_op jit(solution)/shard_map/reduce_scatter | solution.py:103
  860.1 0.8 convert_element_type.25
  860.9 1.1 fusion.7
  862.0 1.0 convolution_subtract_fusion
  863.1 0.3 fusion.26
  863.3 36.0 %reduce-scatter.11.cloned.1.call-done = f32[32,512]{1,0:T(8,128)} async-done(((f32[256,512]{1,0:T(8,128)}), f32[32,512]{1,0:T(8,128)}) %reduce-scatter.11.cloned.1.call-update) | async-done | bytes 65552 | tf_op jit(solution)/shard_map/reduce_scatter | solution.py:109
  899.4 1.5 convert_element_type.27
  900.8 257.2 %all-reduce.8.cloned.1.call-done = f32[256,256]{1,0:T(8,128)} async-done(((f32[256,256]{1,0:T(8,128)}), f32[256,256]{1,0:T(8,128)}) %all-reduce.8.cloned.1.call-update) | async-done | bytes 262160 | tf_op jit(solution)/shard_map/psum | solution.py:123
  1158.1 2.0 fusion.3
  (76 shorter events, 2.1 us)
Async XLA Ops:
  7.2 387.3 %copy-start = (bf16[256,256]{1,0:T(8,128)(2,1)S(1)}, bf16[256,256]{1,0:T(8,128)(2,1)}, u32[]{:S(2)}) copy-start(bf16[256,256]{1,0:T(8,128)(2,1)} %param.19) | copy-start | bytes 393220
  7.2 185.5 %reduce-scatter.5.cloned.1.call-start = ((), (), s32[]{:S(2)}) async-start(), calls=%async_computation.4 | async-start | bytes 2703360 | tf_op jit(solution)/shard_map/reduce_scatter | solution.py:84
  13.3 9.3 copy-start.13
  31.3 3.5 copy-start.8
  67.2 2.8 copy-start.9
  69.9 202.8 %all-gather.3.cloned.1.call-start = ((), (), s32[]{:S(2)}) async-start(), calls=%async_computation.5 | async-start | bytes 1351680 | tf_op jit(solution)/shard_map/all_gather | solution.py:83
  71.2 279.3 %all-reduce.4.cloned.1.call-start = ((), (), s32[]{:S(2)}) async-start(), calls=%async_computation.7 | async-start | bytes 524288 | tf_op jit(solution)/shard_map/psum | solution.py:121
  193.6 136.5 %copy-start.3 = (bf16[80,256]{1,0:T(8,128)(2,1)}, bf16[80,256]{1,0:T(8,128)(2,1)S(1)}, u32[]{:S(2)}) copy-start(bf16[80,256]{1,0:T(8,128)(2,1)S(1)} %convert_element_type.22) | copy-start | bytes 122884
  274.6 3.6 copy-start.12
  274.6 3.7 copy-start.11
  274.6 118.3 %reduce-scatter.7.cloned.1.call-start = ((), (), s32[]{:S(2)}) async-start(), calls=%async_computation.6 | async-start | bytes 737280 | tf_op jit(solution)/shard_map/reduce_scatter | solution.py:90
  278.1 196.4 %all-gather.5.cloned.1.call-start = ((), (), s32[]{:S(2)}) async-start(), calls=%async_computation.10 | async-start | bytes 1081344 | tf_op jit(solution)/shard_map/all_gather | solution.py:97
  279.5 458.1 %all-reduce.6.cloned.1.call-start = ((), (), s32[]{:S(2)}) async-start(), calls=%async_computation.8 | async-start | bytes 524288 | tf_op jit(solution)/shard_map/psum | solution.py:121
  287.3 2.9 copy-start.10
  328.0 2.1 copy-start.2
  350.6 509.5 %reduce-scatter.9.cloned.1.call-start = ((), (), s32[]{:S(2)}) async-start(), calls=%async_computation.9 | async-start | bytes 2162688 | tf_op jit(solution)/shard_map/reduce_scatter | solution.py:103
  354.1 383.5 %copy-start.5 = (f32[256,256]{1,0:T(8,128)S(1)}, f32[256,256]{1,0:T(8,128)}, u32[]{:S(2)}) copy-start(f32[256,256]{1,0:T(8,128)} %param.14) | copy-start | bytes 786436
  354.2 545.2 %reduce-scatter.11.cloned.1.call-start = ((), (), s32[]{:S(2)}) async-start(), calls=%async_computation.11 | async-start | bytes 589824 | tf_op jit(solution)/shard_map/reduce_scatter | solution.py:109
  392.9 84.4 %copy-start.4 = (f32[32,640]{1,0:T(8,128)S(1)}, f32[32,640]{1,0:T(8,128)}, u32[]{:S(2)}) copy-start(f32[32,640]{1,0:T(8,128)} %reduce-scatter.7.cloned.1.call-done) | copy-start | bytes 245764
  477.2 680.8 %copy-start.6 = (f32[256,256]{1,0:T(8,128)S(1)}, f32[256,256]{1,0:T(8,128)}, u32[]{:S(2)}) copy-start(f32[256,256]{1,0:T(8,128)} %param.20) | copy-start | bytes 786436
  477.2 680.8 %all-reduce.8.cloned.1.call-start = ((), (), s32[]{:S(2)}) async-start(), calls=%async_computation.12 | async-start | bytes 524288 | tf_op jit(solution)/shard_map/psum | solution.py:123
  738.6 421.4 %copy-start.1 = (f32[256,256]{1,0:T(8,128)}, f32[256,256]{1,0:T(8,128)S(1)}, u32[]{:S(2)}) copy-start(f32[256,256]{1,0:T(8,128)S(1)} %sub.40) | copy-start | bytes 786436
  860.9 299.1 %copy-start.7 = (bf16[64,256]{1,0:T(8,128)(2,1)}, bf16[64,256]{1,0:T(8,128)(2,1)S(1)}, u32[]{:S(2)}) copy-start(bf16[64,256]{1,0:T(8,128)(2,1)S(1)} %convert_element_type.25) | copy-start | bytes 98308
Sparse Core Ops, SparseCore 0:
  70.0 122.6 reduce-scatter.4
  196.5 76.1 all-gather.2
  276.1 74.4 all-reduce.3
  352.9 39.9 reduce-scatter.6
  396.1 78.2 all-gather.4
  476.9 260.6 all-reduce.5
  742.3 117.6 reduce-scatter.8
  862.6 36.7 reduce-scatter.10
  906.3 251.7 all-reduce.7
